TPU v7x, 32 devices: a whole 2x2x4 slice. The times are simulated.
32 devices in a mesh: section: 4 (over x, core), obs: 8 (over z, y).
Axes of the slice: x: 2, y: 2, z: 4, core: 2. Of those that a mesh axis runs over, the one named last changes fastest.
Arguments:
- predictors: bfloat16 [4, 4, 20, 32768], P('section', None, None, 'obs'), may hold values from -5 to 5
- departures: float32 [4, 4, 32768], P('section', None, 'obs'), may hold values from -30 to 30
- obs_precision: float32 [4, 4, 32768], P('section', None, 'obs'), may hold values from 0.3 to 3
- qc_pass: int32 [4, 4, 32768], P('section', None, 'obs'), may hold values 0 or 1
- block_channel: int32 [4, 4, 256], P('section', None, 'obs'), may hold values from 0 to 2047, as said below
- stream_order: int32 [4], replicated, may hold values from 0 to 3, each once
- prior_coeffs: float32 [4, 20, 2048], P(None, None, 'obs'), may hold values from -1 to 1
- prior_info: float32 [4, 210, 2048], P(None, None, 'obs'), may hold values from -1 to 32, as said below
- memory_factor: float32 [2048], P('obs'), may hold values from 0.5 to 0.98
Outputs:
- coeffs: float32 [4, 4, 20, 2048], P('section', None, None, 'obs')
- information: float32 [4, 4, 210, 2048], P('section', None, None, 'obs')
Inputs may be any that keep to these rules, and one draw needn't show every extreme that they name: `block_channel`: among the 32 row blocks of one index of obs, at most 8 have channels in any one range of the 256 channels from a multiple of 256; in every window and stream one such range holds exactly 8 blocks of every index of obs. `stream_order`: each stream appears once. `prior_info`: for every stream and channel the 210 entries are the upper triangle, row by row, of a symmetric positive definite matrix of order 20.
All inputs are finite; a program needn't handle non-finite values. No bound on the sum of `qc_pass` on one device may be relied on, other than what follows from the above.
Results may differ from a plain program's by a relative error of at most 0.0038.
Values sent between devices are 32-bit elements; how exact they have to be, the bound alone decides.
A program may use at most 64 MiB of HBM per device.

v0:
```python
import jax
import jax.numpy as jnp
import numpy as np
from jax import lax
from jax.sharding import PartitionSpec as P

HUBER_SQ = 9.0
PRIOR_WEIGHT = 64.0


def from_behind(array, axis, by):
    size = lax.axis_size(axis)
    pairs = [(i, i + by) for i in range(size) if 0 <= i + by < size]
    return lax.ppermute(array, axis, pairs)


def upper_positions(dimension):
    return np.array(
        [i * dimension + j for i in range(dimension) for j in range(i, dimension)], dtype=np.int32
    )


def solve_packed(packed, target):
    dimension = target.shape[0]
    placing = {}
    counter = 0
    for i in range(dimension):
        for j in range(i, dimension):
            placing[i, j] = counter
            counter += 1
    factor = [[None] * dimension for i in range(dimension)]
    for j in range(dimension):
        pivot_root = jnp.sqrt(
            packed[placing[j, j]] - sum((factor[j][k] * factor[j][k] for k in range(j)))
        )
        factor[j][j] = pivot_root
        for i in range(j + 1, dimension):
            factor[i][j] = (
                packed[placing[j, i]] - sum((factor[i][k] * factor[j][k] for k in range(j)))
            ) / pivot_root
    forward = []
    for i in range(dimension):
        forward.append(
            (target[i] - sum((factor[i][k] * forward[k] for k in range(i)))) / factor[i][i]
        )
    backward = [None] * dimension
    for i in reversed(range(dimension)):
        backward[i] = (
            forward[i] - sum((factor[k][i] * backward[k] for k in range(i + 1, dimension)))
        ) / factor[i][i]
    return jnp.stack(backward)


def block_terms(predicted, departed, precision, passed, block_coeffs):
    pred_count, row_count = predicted.shape
    block_count = block_coeffs.shape[1]
    block_width = row_count // block_count
    upper_index = upper_positions(pred_count)
    shaped = predicted.reshape(pred_count, block_count, block_width)
    offset = jnp.sum(shaped.astype(jnp.float32) * block_coeffs[:, :, None], axis=0)
    residual = departed.reshape(block_count, block_width) - offset
    scale_row = precision.reshape(block_count, block_width)
    weight = (
        passed.reshape(block_count, block_width).astype(jnp.float32)
        * scale_row
        / (1.0 + scale_row * residual * residual / HUBER_SQ)
    )
    weighted = (weight[None] * shaped.astype(jnp.float32)).astype(jnp.bfloat16)
    chi_square = jnp.sum(weight * residual * residual)
    passed_count = jnp.sum(passed.astype(jnp.float32))
    gram_full = lax.dot_general(
        weighted, shaped, (((2,), (2,)), ((1,), (1,))), preferred_element_type=jnp.float32
    )
    gram_upper = gram_full.reshape(block_count, pred_count * pred_count)[:, upper_index]
    gradient = jnp.sum(weighted.astype(jnp.float32) * residual[None], axis=2).T
    return (jnp.concatenate([gram_upper, gradient], axis=1), jnp.stack([chi_square, passed_count]))


def local(
    predictors,
    departures,
    obs_precision,
    qc_pass,
    block_channel,
    stream_order,
    prior_coeffs,
    prior_info,
    memory_factor,
):
    section_count = lax.axis_size("section")
    obs_devices = lax.axis_size("obs")
    section_place = lax.axis_index("section")
    stream_count = stream_order.shape[0]
    local_channels = memory_factor.shape[0]
    block_count = block_channel.shape[2]
    pred_count = prior_coeffs.shape[1]
    tri_count = prior_info.shape[1]
    column_count = tri_count + pred_count
    capacity = 2 * block_count // obs_devices
    local_line = jnp.arange(local_channels, dtype=jnp.float32)
    owner_line = jnp.arange(obs_devices, dtype=jnp.int32)
    slot_line = jnp.arange(obs_devices * capacity, dtype=jnp.int32)
    highest = lax.Precision.HIGHEST

    def pack_blocks(block_sums, channel):
        owner_index = channel // local_channels
        inner_channel = channel % local_channels
        owner_hot = (owner_index[:, None] == owner_line[None, :]).astype(jnp.int32)
        ranking = jnp.sum((jnp.cumsum(owner_hot, axis=0) - 1) * owner_hot, axis=1)
        slot_of = owner_index * capacity + ranking
        placing = (slot_of[:, None] == slot_line[None, :]).astype(jnp.float32)
        send_rows = lax.dot_general(
            placing,
            block_sums,
            (((0,), (0,)), ((), ())),
            precision=highest,
            preferred_element_type=jnp.float32,
        ).reshape(obs_devices, capacity, column_count)
        send_channel = (
            lax.dot_general(
                placing,
                (inner_channel + 1).astype(jnp.float32),
                (((0,), (0,)), ((), ())),
                precision=highest,
                preferred_element_type=jnp.float32,
            ).reshape(obs_devices, capacity)
            - 1.0
        )
        return (send_rows, send_channel)

    def unpack_blocks(got_rows, got_channel):
        gather_hot = (got_channel.reshape(-1)[:, None] == local_line[None, :]).astype(jnp.float32)
        return lax.dot_general(
            got_rows.reshape(-1, column_count),
            gather_hot,
            (((0,), (0,)), ((), ())),
            precision=highest,
            preferred_element_type=jnp.float32,
        )

    def window_work(state_now, streams):
        beta_prior = state_now[:, :pred_count]
        info_prior = state_now[:, pred_count:]
        all_coeffs = lax.all_gather(beta_prior, "obs", axis=2, tiled=True)
        channel = jnp.take(block_channel[0], streams, axis=0)
        block_coeffs = jax.vmap(lambda coeff_rows, chan: jnp.take(coeff_rows, chan, axis=1))(
            all_coeffs, channel
        )
        block_sums, statistics = jax.vmap(block_terms)(
            jnp.take(predictors[0], streams, axis=0),
            jnp.take(departures[0], streams, axis=0),
            jnp.take(obs_precision[0], streams, axis=0),
            jnp.take(qc_pass[0], streams, axis=0),
            block_coeffs,
        )
        totals = lax.psum(statistics, "obs")
        send_rows, send_channel = jax.vmap(pack_blocks)(block_sums, channel)
        got_rows, got_channel = (
            lax.all_to_all(send_rows, "obs", split_axis=1, concat_axis=1, tiled=True),
            lax.all_to_all(send_channel, "obs", split_axis=1, concat_axis=1, tiled=True),
        )
        normal = jax.vmap(unpack_blocks)(got_rows, got_channel)
        inflation = (totals[:, 0] + PRIOR_WEIGHT) / (totals[:, 1] + PRIOR_WEIGHT)
        info_post = info_prior + normal[:, :tri_count] / inflation[:, None, None]
        beta_post = beta_prior + jax.vmap(solve_packed)(
            info_post, normal[:, tri_count:] / inflation[:, None, None]
        )
        outgoing = jnp.concatenate([beta_post, memory_factor[None, None, :] * info_post], axis=1)
        incoming = from_behind(outgoing, "section", 1)
        return (beta_post, info_post, incoming)

    def fresh_of(streams):
        return jnp.concatenate(
            [jnp.take(prior_coeffs, streams, axis=0), jnp.take(prior_info, streams, axis=0)], axis=1
        )

    coeff_start = jnp.zeros((1, stream_count, pred_count, local_channels), jnp.float32)
    info_start = jnp.zeros((1, stream_count, tri_count, local_channels), jnp.float32)

    def tick_step(t, loop_state):
        incoming, coeff_out, info_out = loop_state
        entry_index = t - section_place
        usable = (entry_index >= 0) & (entry_index < stream_count)
        slot_index = jnp.clip(entry_index, 0, stream_count - 1)
        streams = lax.dynamic_slice_in_dim(stream_order, slot_index, 1, 0)
        state_now = jnp.where(
            (section_place == 0) | jnp.logical_not(usable), fresh_of(streams), incoming
        )
        beta_post, info_post, incoming = window_work(state_now, streams)

        def store_entry(buffer, result):
            current = lax.dynamic_slice_in_dim(buffer, slot_index, 1, 1)
            updated = jnp.where(usable, result[None], current)
            return lax.dynamic_update_slice_in_dim(buffer, updated, slot_index, 1)

        return (incoming, store_entry(coeff_out, beta_post), store_entry(info_out, info_post))

    initial = (jnp.zeros((1, column_count, local_channels), jnp.float32), coeff_start, info_start)
    final_state = lax.fori_loop(0, stream_count + section_count - 1, tick_step, initial)
    return (final_state[1], final_state[2])


def solution(mesh):
    in_specs = (
        P("section", None, None, "obs"),
        P("section", None, "obs"),
        P("section", None, "obs"),
        P("section", None, "obs"),
        P("section", None, "obs"),
        P(),
        P(None, None, "obs"),
        P(None, None, "obs"),
        P("obs"),
    )
    out_specs = (P("section", None, None, "obs"), P("section", None, None, "obs"))
    return jax.shard_map(local, mesh=mesh, in_specs=in_specs, out_specs=out_specs, check_vma=False)
```

profile of v0, /device:TPU:1, one launch (start us, length us, event | category | flops | bytes accessed | tf_op | source)
XLA Modules:
  0.0 688.5 jit_solution(5905409147109336993)
XLA Ops:
  2.9 684.6 %while.38 = (s32[]{:T(128)}, f32[1,230,256]{2,1,0:T(8,128)S(1)}, f32[1,4,20,256]{3,1,2,0:T(4,128)S(1)}, f32[1,4,210,256]{3,1,2,0:T(4,128)S(1)}, s32[]{:T(128)}, ...) while((s32[]{:T(128)}, f32[1,230,256]{2,1,0:T(8,128)S(1)}, ...), condition=%wide.region_8.10_spmd.clone.clone, body=%wide.region_0.9_spmd.sunk.clone.clone.sunk | while | flops 57759508 | bytes 13853709 | solution.py:199
  7.5 6.4 all-to-all-start.1
  16.3 24.6 %all_gather.15 = f32[1,20,2048]{2,1,0:T(8,128)S(1)} all-gather(f32[1,20,256]{2,1,0:T(8,128)S(1)} %slice.5342), channel_id=1, replica_groups=mesh['section'=4,'obs'=8] {'obs'}, dimensions={2}, use_global_device_ids=true | all-gather | bytes 184320 | tf_op jit(solution)/shard_map/while/body/eval_jaxpr/all_gather | solution.py:144
  47.6 17.5 %psum.19 = f32[1,2]{1,0:T(1,128)S(1)} all-reduce(f32[1,2]{1,0:T(1,128)S(1)} %maximum_bitcast_fusion.6), channel_id=1, replica_groups=mesh['section'=4,'obs'=8] {'obs'}, use_global_device_ids=true, to_apply=%region_7.8 | all-reduce | flops 2 | bytes 16 | tf_op jit(solution)/shard_map/while/body/eval_jaxpr/psum | solution.py:156
  68.0 3.4 all-to-all-start
  72.6 4.4 all-to-all-done
  83.2 15.7 %collective-permute-start = (f32[1,230,256]{2,1,0:T(8,128)S(1)}, f32[1,230,256]{2,1,0:T(8,128)S(1)}, u32[]{:S(2)}, u32[]{:S(2)}) collective-permute-start(f32[1,230,256]{2,1,0:T(8,128)S(1)} %pad_maximum_fusion.2), channel_id=1, source_target_pairs={{0,8},{8,16},{16,24},{1,9},{9,17},{17,25},{2,10},{10,18},{18,26},{... | collective-permute-start | bytes 706568 | tf_op jit(solution)/shard_map/while/body/eval_jaxpr/ppermute | solution.py:14
  99.3 5.9 dynamic_update_slice.31
  109.8 3.3 all-to-all-start.1
  115.6 25.2 %all_gather.15 = f32[1,20,2048]{2,1,0:T(8,128)S(1)} all-gather(f32[1,20,256]{2,1,0:T(8,128)S(1)} %slice.5342), channel_id=1, replica_groups=mesh['section'=4,'obs'=8] {'obs'}, dimensions={2}, use_global_device_ids=true | all-gather | bytes 184320 | tf_op jit(solution)/shard_map/while/body/eval_jaxpr/all_gather | solution.py:144
  147.5 17.3 %psum.19 = f32[1,2]{1,0:T(1,128)S(1)} all-reduce(f32[1,2]{1,0:T(1,128)S(1)} %maximum_bitcast_fusion.6), channel_id=1, replica_groups=mesh['section'=4,'obs'=8] {'obs'}, use_global_device_ids=true, to_apply=%region_7.8 | all-reduce | flops 2 | bytes 16 | tf_op jit(solution)/shard_map/while/body/eval_jaxpr/psum | solution.py:156
  167.6 3.4 all-to-all-start
  172.3 4.4 all-to-all-done
  182.9 13.1 %collective-permute-start = (f32[1,230,256]{2,1,0:T(8,128)S(1)}, f32[1,230,256]{2,1,0:T(8,128)S(1)}, u32[]{:S(2)}, u32[]{:S(2)}) collective-permute-start(f32[1,230,256]{2,1,0:T(8,128)S(1)} %pad_maximum_fusion.2), channel_id=1, source_target_pairs={{0,8},{8,16},{16,24},{1,9},{9,17},{17,25},{2,10},{10,18},{18,26},{... | collective-permute-start | bytes 706568 | tf_op jit(solution)/shard_map/while/body/eval_jaxpr/ppermute | solution.py:14
  196.4 5.9 dynamic_update_slice.31
  206.9 3.3 all-to-all-start.1
  212.6 24.6 %all_gather.15 = f32[1,20,2048]{2,1,0:T(8,128)S(1)} all-gather(f32[1,20,256]{2,1,0:T(8,128)S(1)} %slice.5342), channel_id=1, replica_groups=mesh['section'=4,'obs'=8] {'obs'}, dimensions={2}, use_global_device_ids=true | all-gather | bytes 184320 | tf_op jit(solution)/shard_map/while/body/eval_jaxpr/all_gather | solution.py:144
  244.0 17.5 %psum.19 = f32[1,2]{1,0:T(1,128)S(1)} all-reduce(f32[1,2]{1,0:T(1,128)S(1)} %maximum_bitcast_fusion.6), channel_id=1, replica_groups=mesh['section'=4,'obs'=8] {'obs'}, use_global_device_ids=true, to_apply=%region_7.8 | all-reduce | flops 2 | bytes 16 | tf_op jit(solution)/shard_map/while/body/eval_jaxpr/psum | solution.py:156
  264.4 3.4 all-to-all-start
  269.0 4.4 all-to-all-done
  279.6 13.4 %collective-permute-start = (f32[1,230,256]{2,1,0:T(8,128)S(1)}, f32[1,230,256]{2,1,0:T(8,128)S(1)}, u32[]{:S(2)}, u32[]{:S(2)}) collective-permute-start(f32[1,230,256]{2,1,0:T(8,128)S(1)} %pad_maximum_fusion.2), channel_id=1, source_target_pairs={{0,8},{8,16},{16,24},{1,9},{9,17},{17,25},{2,10},{10,18},{18,26},{... | collective-permute-start | bytes 706568 | tf_op jit(solution)/shard_map/while/body/eval_jaxpr/ppermute | solution.py:14
  293.4 5.9 dynamic_update_slice.31
  303.9 3.3 all-to-all-start.1
  309.7 24.8 %all_gather.15 = f32[1,20,2048]{2,1,0:T(8,128)S(1)} all-gather(f32[1,20,256]{2,1,0:T(8,128)S(1)} %slice.5342), channel_id=1, replica_groups=mesh['section'=4,'obs'=8] {'obs'}, dimensions={2}, use_global_device_ids=true | all-gather | bytes 184320 | tf_op jit(solution)/shard_map/while/body/eval_jaxpr/all_gather | solution.py:144
  341.3 17.6 %psum.19 = f32[1,2]{1,0:T(1,128)S(1)} all-reduce(f32[1,2]{1,0:T(1,128)S(1)} %maximum_bitcast_fusion.6), channel_id=1, replica_groups=mesh['section'=4,'obs'=8] {'obs'}, use_global_device_ids=true, to_apply=%region_7.8 | all-reduce | flops 2 | bytes 16 | tf_op jit(solution)/shard_map/while/body/eval_jaxpr/psum | solution.py:156
  361.8 3.4 all-to-all-start
  366.4 4.4 all-to-all-done
  377.0 13.1 %collective-permute-start = (f32[1,230,256]{2,1,0:T(8,128)S(1)}, f32[1,230,256]{2,1,0:T(8,128)S(1)}, u32[]{:S(2)}, u32[]{:S(2)}) collective-permute-start(f32[1,230,256]{2,1,0:T(8,128)S(1)} %pad_maximum_fusion.2), channel_id=1, source_target_pairs={{0,8},{8,16},{16,24},{1,9},{9,17},{17,25},{2,10},{10,18},{18,26},{... | collective-permute-start | bytes 706568 | tf_op jit(solution)/shard_map/while/body/eval_jaxpr/ppermute | solution.py:14
  390.5 5.9 dynamic_update_slice.31
  401.0 3.3 all-to-all-start.1
  406.7 24.9 %all_gather.15 = f32[1,20,2048]{2,1,0:T(8,128)S(1)} all-gather(f32[1,20,256]{2,1,0:T(8,128)S(1)} %slice.5342), channel_id=1, replica_groups=mesh['section'=4,'obs'=8] {'obs'}, dimensions={2}, use_global_device_ids=true | all-gather | bytes 184320 | tf_op jit(solution)/shard_map/while/body/eval_jaxpr/all_gather | solution.py:144
  438.4 17.2 %psum.19 = f32[1,2]{1,0:T(1,128)S(1)} all-reduce(f32[1,2]{1,0:T(1,128)S(1)} %maximum_bitcast_fusion.6), channel_id=1, replica_groups=mesh['section'=4,'obs'=8] {'obs'}, use_global_device_ids=true, to_apply=%region_7.8 | all-reduce | flops 2 | bytes 16 | tf_op jit(solution)/shard_map/while/body/eval_jaxpr/psum | solution.py:156
  458.5 3.4 all-to-all-start
  463.2 4.4 all-to-all-done
  473.8 13.4 %collective-permute-start = (f32[1,230,256]{2,1,0:T(8,128)S(1)}, f32[1,230,256]{2,1,0:T(8,128)S(1)}, u32[]{:S(2)}, u32[]{:S(2)}) collective-permute-start(f32[1,230,256]{2,1,0:T(8,128)S(1)} %pad_maximum_fusion.2), channel_id=1, source_target_pairs={{0,8},{8,16},{16,24},{1,9},{9,17},{17,25},{2,10},{10,18},{18,26},{... | collective-permute-start | bytes 706568 | tf_op jit(solution)/shard_map/while/body/eval_jaxpr/ppermute | solution.py:14
  487.5 5.9 dynamic_update_slice.31
  503.8 24.8 %all_gather.15 = f32[1,20,2048]{2,1,0:T(8,128)S(1)} all-gather(f32[1,20,256]{2,1,0:T(8,128)S(1)} %slice.5342), channel_id=1, replica_groups=mesh['section'=4,'obs'=8] {'obs'}, dimensions={2}, use_global_device_ids=true | all-gather | bytes 184320 | tf_op jit(solution)/shard_map/while/body/eval_jaxpr/all_gather | solution.py:144
  535.4 17.5 %psum.19 = f32[1,2]{1,0:T(1,128)S(1)} all-reduce(f32[1,2]{1,0:T(1,128)S(1)} %maximum_bitcast_fusion.6), channel_id=1, replica_groups=mesh['section'=4,'obs'=8] {'obs'}, use_global_device_ids=true, to_apply=%region_7.8 | all-reduce | flops 2 | bytes 16 | tf_op jit(solution)/shard_map/while/body/eval_jaxpr/psum | solution.py:156
  555.8 3.4 all-to-all-start
  560.4 4.4 all-to-all-done
  571.0 13.2 %collective-permute-start = (f32[1,230,256]{2,1,0:T(8,128)S(1)}, f32[1,230,256]{2,1,0:T(8,128)S(1)}, u32[]{:S(2)}, u32[]{:S(2)}) collective-permute-start(f32[1,230,256]{2,1,0:T(8,128)S(1)} %pad_maximum_fusion.2), channel_id=1, source_target_pairs={{0,8},{8,16},{16,24},{1,9},{9,17},{17,25},{2,10},{10,18},{18,26},{... | collective-permute-start | bytes 706568 | tf_op jit(solution)/shard_map/while/body/eval_jaxpr/ppermute | solution.py:14
  584.6 5.9 dynamic_update_slice.31
  600.9 24.5 %all_gather.15 = f32[1,20,2048]{2,1,0:T(8,128)S(1)} all-gather(f32[1,20,256]{2,1,0:T(8,128)S(1)} %slice.5342), channel_id=1, replica_groups=mesh['section'=4,'obs'=8] {'obs'}, dimensions={2}, use_global_device_ids=true | all-gather | bytes 184320 | tf_op jit(solution)/shard_map/while/body/eval_jaxpr/all_gather | solution.py:144
  632.1 18.0 %psum.19 = f32[1,2]{1,0:T(1,128)S(1)} all-reduce(f32[1,2]{1,0:T(1,128)S(1)} %maximum_bitcast_fusion.6), channel_id=1, replica_groups=mesh['section'=4,'obs'=8] {'obs'}, use_global_device_ids=true, to_apply=%region_7.8 | all-reduce | flops 2 | bytes 16 | tf_op jit(solution)/shard_map/while/body/eval_jaxpr/psum | solution.py:156
  652.9 3.4 all-to-all-start
  657.6 4.4 all-to-all-done
  668.2 13.1 %collective-permute-start = (f32[1,230,256]{2,1,0:T(8,128)S(1)}, f32[1,230,256]{2,1,0:T(8,128)S(1)}, u32[]{:S(2)}, u32[]{:S(2)}) collective-permute-start(f32[1,230,256]{2,1,0:T(8,128)S(1)} %pad_maximum_fusion.2), channel_id=1, source_target_pairs={{0,8},{8,16},{16,24},{1,9},{9,17},{17,25},{2,10},{10,18},{18,26},{... | collective-permute-start | bytes 706568 | tf_op jit(solution)/shard_map/while/body/eval_jaxpr/ppermute | solution.py:14
  681.7 5.9 dynamic_update_slice.31
  (632 shorter events, 155.7 us)
Async XLA Ops:
  2.2 0.7 copy-start.4
  2.3 0.7 copy-start.5
  2.3 0.7 copy-start.6
  7.5 60.4 %all-to-all-start.1 = ((f32[1,8,8]{2,0,1:T(1,128)}), f32[1,8,8]{2,0,1:T(1,128)S(1)}, u32[]{:S(2)}, u32[]{:S(2)}) async-start(f32[1,8,8]{2,0,1:T(1,128)} %bitcast.2454), calls=%async_computation.1 | async-start | bytes 8192 | tf_op jit(solution)/shard_map/while/body/eval_jaxpr/all_to_all | solution.py:160
  68.0 9.1 %all-to-all-start = ((f32[1,8,8,230]{3,2,0,1:T(8,128)}), f32[1,8,8,230]{3,2,0,1:T(8,128)S(1)}, u32[]{:S(2)}, u32[]{:S(2)}) async-start(f32[1,8,8,230]{3,2,0,1:T(8,128)} %convolution_bitcast_fusion.4), calls=%async_computation | async-start | bytes 131072 | tf_op jit(solution)/shard_map/while/body/eval_jaxpr/all_to_all | solution.py:159
  77.4 0.6 copy-start
  78.8 0.7 slice-start
  80.7 0.7 copy-start.1
  83.2 22.0 %collective-permute-start = (f32[1,230,256]{2,1,0:T(8,128)S(1)}, f32[1,230,256]{2,1,0:T(8,128)S(1)}, u32[]{:S(2)}, u32[]{:S(2)}) collective-permute-start(f32[1,230,256]{2,1,0:T(8,128)S(1)} %pad_maximum_fusion.2), channel_id=1, source_target_pairs={{0,8},{8,16},{16,24},{1,9},{9,17},{17,25},{2,10},{10,18},{18,26},{... | collective-permute-start | bytes 706568 | tf_op jit(solution)/shard_map/while/body/eval_jaxpr/ppermute | solution.py:14
  109.8 57.8 %all-to-all-start.1 = ((f32[1,8,8]{2,0,1:T(1,128)}), f32[1,8,8]{2,0,1:T(1,128)S(1)}, u32[]{:S(2)}, u32[]{:S(2)}) async-start(f32[1,8,8]{2,0,1:T(1,128)} %bitcast.2454), calls=%async_computation.1 | async-start | bytes 8192 | tf_op jit(solution)/shard_map/while/body/eval_jaxpr/all_to_all | solution.py:160
  167.6 9.1 %all-to-all-start = ((f32[1,8,8,230]{3,2,0,1:T(8,128)}), f32[1,8,8,230]{3,2,0,1:T(8,128)S(1)}, u32[]{:S(2)}, u32[]{:S(2)}) async-start(f32[1,8,8,230]{3,2,0,1:T(8,128)} %convolution_bitcast_fusion.4), calls=%async_computation | async-start | bytes 131072 | tf_op jit(solution)/shard_map/while/body/eval_jaxpr/all_to_all | solution.py:159
  177.1 0.6 copy-start
  178.5 0.7 slice-start
  180.4 0.7 copy-start.1
  182.9 19.4 %collective-permute-start = (f32[1,230,256]{2,1,0:T(8,128)S(1)}, f32[1,230,256]{2,1,0:T(8,128)S(1)}, u32[]{:S(2)}, u32[]{:S(2)}) collective-permute-start(f32[1,230,256]{2,1,0:T(8,128)S(1)} %pad_maximum_fusion.2), channel_id=1, source_target_pairs={{0,8},{8,16},{16,24},{1,9},{9,17},{17,25},{2,10},{10,18},{18,26},{... | collective-permute-start | bytes 706568 | tf_op jit(solution)/shard_map/while/body/eval_jaxpr/ppermute | solution.py:14
  206.9 57.5 %all-to-all-start.1 = ((f32[1,8,8]{2,0,1:T(1,128)}), f32[1,8,8]{2,0,1:T(1,128)S(1)}, u32[]{:S(2)}, u32[]{:S(2)}) async-start(f32[1,8,8]{2,0,1:T(1,128)} %bitcast.2454), calls=%async_computation.1 | async-start | bytes 8192 | tf_op jit(solution)/shard_map/while/body/eval_jaxpr/all_to_all | solution.py:160
  264.4 9.1 %all-to-all-start = ((f32[1,8,8,230]{3,2,0,1:T(8,128)}), f32[1,8,8,230]{3,2,0,1:T(8,128)S(1)}, u32[]{:S(2)}, u32[]{:S(2)}) async-start(f32[1,8,8,230]{3,2,0,1:T(8,128)} %convolution_bitcast_fusion.4), calls=%async_computation | async-start | bytes 131072 | tf_op jit(solution)/shard_map/while/body/eval_jaxpr/all_to_all | solution.py:159
  273.8 0.6 copy-start
  275.2 0.7 slice-start
  277.1 0.7 copy-start.1
  279.6 19.7 %collective-permute-start = (f32[1,230,256]{2,1,0:T(8,128)S(1)}, f32[1,230,256]{2,1,0:T(8,128)S(1)}, u32[]{:S(2)}, u32[]{:S(2)}) collective-permute-start(f32[1,230,256]{2,1,0:T(8,128)S(1)} %pad_maximum_fusion.2), channel_id=1, source_target_pairs={{0,8},{8,16},{16,24},{1,9},{9,17},{17,25},{2,10},{10,18},{18,26},{... | collective-permute-start | bytes 706568 | tf_op jit(solution)/shard_map/while/body/eval_jaxpr/ppermute | solution.py:14
  303.9 57.8 %all-to-all-start.1 = ((f32[1,8,8]{2,0,1:T(1,128)}), f32[1,8,8]{2,0,1:T(1,128)S(1)}, u32[]{:S(2)}, u32[]{:S(2)}) async-start(f32[1,8,8]{2,0,1:T(1,128)} %bitcast.2454), calls=%async_computation.1 | async-start | bytes 8192 | tf_op jit(solution)/shard_map/while/body/eval_jaxpr/all_to_all | solution.py:160
  361.8 9.1 %all-to-all-start = ((f32[1,8,8,230]{3,2,0,1:T(8,128)}), f32[1,8,8,230]{3,2,0,1:T(8,128)S(1)}, u32[]{:S(2)}, u32[]{:S(2)}) async-start(f32[1,8,8,230]{3,2,0,1:T(8,128)} %convolution_bitcast_fusion.4), calls=%async_computation | async-start | bytes 131072 | tf_op jit(solution)/shard_map/while/body/eval_jaxpr/all_to_all | solution.py:159
  371.2 0.6 copy-start
  372.6 0.7 slice-start
  374.5 0.7 copy-start.1
  377.0 19.4 %collective-permute-start = (f32[1,230,256]{2,1,0:T(8,128)S(1)}, f32[1,230,256]{2,1,0:T(8,128)S(1)}, u32[]{:S(2)}, u32[]{:S(2)}) collective-permute-start(f32[1,230,256]{2,1,0:T(8,128)S(1)} %pad_maximum_fusion.2), channel_id=1, source_target_pairs={{0,8},{8,16},{16,24},{1,9},{9,17},{17,25},{2,10},{10,18},{18,26},{... | collective-permute-start | bytes 706568 | tf_op jit(solution)/shard_map/while/body/eval_jaxpr/ppermute | solution.py:14
  401.0 57.5 %all-to-all-start.1 = ((f32[1,8,8]{2,0,1:T(1,128)}), f32[1,8,8]{2,0,1:T(1,128)S(1)}, u32[]{:S(2)}, u32[]{:S(2)}) async-start(f32[1,8,8]{2,0,1:T(1,128)} %bitcast.2454), calls=%async_computation.1 | async-start | bytes 8192 | tf_op jit(solution)/shard_map/while/body/eval_jaxpr/all_to_all | solution.py:160
  458.5 9.1 %all-to-all-start = ((f32[1,8,8,230]{3,2,0,1:T(8,128)}), f32[1,8,8,230]{3,2,0,1:T(8,128)S(1)}, u32[]{:S(2)}, u32[]{:S(2)}) async-start(f32[1,8,8,230]{3,2,0,1:T(8,128)} %convolution_bitcast_fusion.4), calls=%async_computation | async-start | bytes 131072 | tf_op jit(solution)/shard_map/while/body/eval_jaxpr/all_to_all | solution.py:159
  468.0 0.6 copy-start
  469.4 0.7 slice-start
  471.3 0.7 copy-start.1
  473.8 19.7 %collective-permute-start = (f32[1,230,256]{2,1,0:T(8,128)S(1)}, f32[1,230,256]{2,1,0:T(8,128)S(1)}, u32[]{:S(2)}, u32[]{:S(2)}) collective-permute-start(f32[1,230,256]{2,1,0:T(8,128)S(1)} %pad_maximum_fusion.2), channel_id=1, source_target_pairs={{0,8},{8,16},{16,24},{1,9},{9,17},{17,25},{2,10},{10,18},{18,26},{... | collective-permute-start | bytes 706568 | tf_op jit(solution)/shard_map/while/body/eval_jaxpr/ppermute | solution.py:14
  498.1 57.7 %all-to-all-start.1 = ((f32[1,8,8]{2,0,1:T(1,128)}), f32[1,8,8]{2,0,1:T(1,128)S(1)}, u32[]{:S(2)}, u32[]{:S(2)}) async-start(f32[1,8,8]{2,0,1:T(1,128)} %bitcast.2454), calls=%async_computation.1 | async-start | bytes 8192 | tf_op jit(solution)/shard_map/while/body/eval_jaxpr/all_to_all | solution.py:160
  555.8 9.1 %all-to-all-start = ((f32[1,8,8,230]{3,2,0,1:T(8,128)}), f32[1,8,8,230]{3,2,0,1:T(8,128)S(1)}, u32[]{:S(2)}, u32[]{:S(2)}) async-start(f32[1,8,8,230]{3,2,0,1:T(8,128)} %convolution_bitcast_fusion.4), calls=%async_computation | async-start | bytes 131072 | tf_op jit(solution)/shard_map/while/body/eval_jaxpr/all_to_all | solution.py:159
  565.2 0.6 copy-start
  566.6 0.7 slice-start
  568.5 0.7 copy-start.1
  571.0 19.5 %collective-permute-start = (f32[1,230,256]{2,1,0:T(8,128)S(1)}, f32[1,230,256]{2,1,0:T(8,128)S(1)}, u32[]{:S(2)}, u32[]{:S(2)}) collective-permute-start(f32[1,230,256]{2,1,0:T(8,128)S(1)} %pad_maximum_fusion.2), channel_id=1, source_target_pairs={{0,8},{8,16},{16,24},{1,9},{9,17},{17,25},{2,10},{10,18},{18,26},{... | collective-permute-start | bytes 706568 | tf_op jit(solution)/shard_map/while/body/eval_jaxpr/ppermute | solution.py:14
  595.1 57.8 %all-to-all-start.1 = ((f32[1,8,8]{2,0,1:T(1,128)}), f32[1,8,8]{2,0,1:T(1,128)S(1)}, u32[]{:S(2)}, u32[]{:S(2)}) async-start(f32[1,8,8]{2,0,1:T(1,128)} %bitcast.2454), calls=%async_computation.1 | async-start | bytes 8192 | tf_op jit(solution)/shard_map/while/body/eval_jaxpr/all_to_all | solution.py:160
  652.9 9.1 %all-to-all-start = ((f32[1,8,8,230]{3,2,0,1:T(8,128)}), f32[1,8,8,230]{3,2,0,1:T(8,128)S(1)}, u32[]{:S(2)}, u32[]{:S(2)}) async-start(f32[1,8,8,230]{3,2,0,1:T(8,128)} %convolution_bitcast_fusion.4), calls=%async_computation | async-start | bytes 131072 | tf_op jit(solution)/shard_map/while/body/eval_jaxpr/all_to_all | solution.py:159
  662.4 0.6 copy-start
  663.8 0.7 slice-start
  665.7 0.7 copy-start.1
  668.2 19.4 %collective-permute-start = (f32[1,230,256]{2,1,0:T(8,128)S(1)}, f32[1,230,256]{2,1,0:T(8,128)S(1)}, u32[]{:S(2)}, u32[]{:S(2)}) collective-permute-start(f32[1,230,256]{2,1,0:T(8,128)S(1)} %pad_maximum_fusion.2), channel_id=1, source_target_pairs={{0,8},{8,16},{16,24},{1,9},{9,17},{17,25},{2,10},{10,18},{18,26},{... | collective-permute-start | bytes 706568 | tf_op jit(solution)/shard_map/while/body/eval_jaxpr/ppermute | solution.py:14
  687.6 0.9 copy-start.2
  687.6 0.9 copy-start.3
where the time goes:
time: 692 us; the launch traced here: 689 us
  blocking collectives  296 us (43%)
  starting transfers between devices  145 us (21%)
  local copies, waits for them, and re-layouts  109 us (16%)
  other arithmetic  68.2 us (10%)
  waiting for transfers between devices  30.8 us (4%)
  loops' own time  25.7 us (4%)
  matrix products  12.9 us (2%)
    all_gather x7, blocking collectives, window_work(): all_coeffs = lax.all_gather(beta_prior, 'obs', axis=2, tiled=True)  173 us
    psum x7, blocking collectives, window_work(): totals = lax.psum(statistics, 'obs')  123 us
    ppermute x7, starting transfers between devices, from_behind(): return lax.ppermute(array, axis, pairs)  95 us
    dynamic_update_slice x28, local copies, waits for them, and re-layouts, store_entry(): return lax.dynamic_update_slice_in_dim(buffer, updated, slot_index, 1)  43.8 us
    all_to_all x7, waiting for transfers between devices, window_work(): lax.all_to_all(send_rows, 'obs', split_axis=1, concat_axis=1, tiled=True)  30.8 us
    all_to_all x7, starting transfers between devices, window_work(): lax.all_to_all(send_channel, 'obs', split_axis=1, concat_axis=1, tiled=True)  26.2 us
    another operation x1, loops' own time, local(): lax.fori_loop(0, stream_count + section_count - 1, tick_step, initial)  25.7 us
    all_to_all x7, starting transfers between devices, window_work(): lax.all_to_all(send_rows, 'obs', split_axis=1, concat_axis=1, tiled=True)  23.5 us
  transfers between devices with their start and end apart: 21, of which 7 were waited for; matrix products, arithmetic and copies ran while one was open for 18% of the time, Pallas kernels for 0%

commit v1 on v0

--- a/solution.py
+++ b/solution.py
@@ -141,7 +141,8 @@
     def window_work(state_now, streams):
         beta_prior = state_now[:, :pred_count]
         info_prior = state_now[:, pred_count:]
-        all_coeffs = lax.all_gather(beta_prior, "obs", axis=2, tiled=True)
+        pieces = lax.all_gather(beta_prior, "obs")
+        all_coeffs = jnp.concatenate(pieces, axis=2)
         channel = jnp.take(block_channel[0], streams, axis=0)
         block_coeffs = jax.vmap(lambda coeff_rows, chan: jnp.take(coeff_rows, chan, axis=1))(
             all_coeffs, channel

time: 692 us -> 692 us (level)
  no operation moved by 1% of the time
where the time goes in v1:
time: 692 us; the launch traced here: 689 us
  blocking collectives  296 us (43%)
  starting transfers between devices  145 us (21%)
  local copies, waits for them, and re-layouts  109 us (16%)
  other arithmetic  68.2 us (10%)
  waiting for transfers between devices  30.8 us (4%)
  loops' own time  25.7 us (4%)
  matrix products  12.9 us (2%)
    all_gather x7, blocking collectives, window_work(): pieces = lax.all_gather(beta_prior, 'obs')  173 us
    psum x7, blocking collectives, window_work(): totals = lax.psum(statistics, 'obs')  123 us
    ppermute x7, starting transfers between devices, from_behind(): return lax.ppermute(array, axis, pairs)  95 us
    dynamic_update_slice x28, local copies, waits for them, and re-layouts, store_entry(): return lax.dynamic_update_slice_in_dim(buffer, updated, slot_index, 1)  43.8 us
    all_to_all x7, waiting for transfers between devices, window_work(): lax.all_to_all(send_rows, 'obs', split_axis=1, concat_axis=1, tiled=True)  30.8 us
    all_to_all x7, starting transfers between devices, window_work(): lax.all_to_all(send_channel, 'obs', split_axis=1, concat_axis=1, tiled=True)  26.2 us
    another operation x1, loops' own time, local(): lax.fori_loop(0, stream_count + section_count - 1, tick_step, initial)  25.7 us
    all_to_all x7, starting transfers between devices, window_work(): lax.all_to_all(send_rows, 'obs', split_axis=1, concat_axis=1, tiled=True)  23.5 us
  transfers between devices with their start and end apart: 21, of which 7 were waited for; matrix products, arithmetic and copies ran while one was open for 18% of the time, Pallas kernels for 0%

profile of v1, /device:TPU:1, one launch (start us, length us, event | category | flops | bytes accessed | tf_op | source)
XLA Modules:
  0.0 688.5 jit_solution(9051573476740157524)
XLA Ops:
  2.9 684.6 %while.38 = (s32[]{:T(128)}, f32[1,230,256]{2,1,0:T(8,128)S(1)}, f32[1,4,20,256]{3,1,2,0:T(4,128)S(1)}, f32[1,4,210,256]{3,1,2,0:T(4,128)S(1)}, s32[]{:T(128)}, ...) while((s32[]{:T(128)}, f32[1,230,256]{2,1,0:T(8,128)S(1)}, ...), condition=%wide.region_8.10_spmd.clone.clone, body=%wide.region_0.9_spmd.sunk.clone.clone.sunk | while | flops 57759508 | bytes 13853709 | solution.py:200
  7.5 6.4 all-to-all-start.1
  16.3 24.6 %all-gather.3 = f32[8,20,256]{2,1,0:T(8,128)S(1)} all-gather(f32[1,20,256]{2,1,0:T(8,128)S(1)} %slice.5342), channel_id=2, replica_groups=mesh['section'=4,'obs'=8] {'obs'}, dimensions={0}, use_global_device_ids=true | all-gather | bytes 184320 | tf_op jit(solution)/shard_map/while/body/eval_jaxpr/all_gather | solution.py:144
  47.6 17.5 %psum.19 = f32[1,2]{1,0:T(1,128)S(1)} all-reduce(f32[1,2]{1,0:T(1,128)S(1)} %maximum_bitcast_fusion.6), channel_id=1, replica_groups=mesh['section'=4,'obs'=8] {'obs'}, use_global_device_ids=true, to_apply=%region_7.8 | all-reduce | flops 2 | bytes 16 | tf_op jit(solution)/shard_map/while/body/eval_jaxpr/psum | solution.py:157
  68.0 3.4 all-to-all-start
  72.6 4.4 all-to-all-done
  83.2 15.7 %collective-permute-start = (f32[1,230,256]{2,1,0:T(8,128)S(1)}, f32[1,230,256]{2,1,0:T(8,128)S(1)}, u32[]{:S(2)}, u32[]{:S(2)}) collective-permute-start(f32[1,230,256]{2,1,0:T(8,128)S(1)} %pad_maximum_fusion.2), channel_id=1, source_target_pairs={{0,8},{8,16},{16,24},{1,9},{9,17},{17,25},{2,10},{10,18},{18,26},{... | collective-permute-start | bytes 706568 | tf_op jit(solution)/shard_map/while/body/eval_jaxpr/ppermute | solution.py:14
  99.3 5.9 dynamic_update_slice.31
  109.8 3.3 all-to-all-start.1
  115.6 25.2 %all-gather.3 = f32[8,20,256]{2,1,0:T(8,128)S(1)} all-gather(f32[1,20,256]{2,1,0:T(8,128)S(1)} %slice.5342), channel_id=2, replica_groups=mesh['section'=4,'obs'=8] {'obs'}, dimensions={0}, use_global_device_ids=true | all-gather | bytes 184320 | tf_op jit(solution)/shard_map/while/body/eval_jaxpr/all_gather | solution.py:144
  147.5 17.3 %psum.19 = f32[1,2]{1,0:T(1,128)S(1)} all-reduce(f32[1,2]{1,0:T(1,128)S(1)} %maximum_bitcast_fusion.6), channel_id=1, replica_groups=mesh['section'=4,'obs'=8] {'obs'}, use_global_device_ids=true, to_apply=%region_7.8 | all-reduce | flops 2 | bytes 16 | tf_op jit(solution)/shard_map/while/body/eval_jaxpr/psum | solution.py:157
  167.6 3.4 all-to-all-start
  172.3 4.4 all-to-all-done
  182.9 13.1 %collective-permute-start = (f32[1,230,256]{2,1,0:T(8,128)S(1)}, f32[1,230,256]{2,1,0:T(8,128)S(1)}, u32[]{:S(2)}, u32[]{:S(2)}) collective-permute-start(f32[1,230,256]{2,1,0:T(8,128)S(1)} %pad_maximum_fusion.2), channel_id=1, source_target_pairs={{0,8},{8,16},{16,24},{1,9},{9,17},{17,25},{2,10},{10,18},{18,26},{... | collective-permute-start | bytes 706568 | tf_op jit(solution)/shard_map/while/body/eval_jaxpr/ppermute | solution.py:14
  196.4 5.9 dynamic_update_slice.31
  206.9 3.3 all-to-all-start.1
  212.6 24.6 %all-gather.3 = f32[8,20,256]{2,1,0:T(8,128)S(1)} all-gather(f32[1,20,256]{2,1,0:T(8,128)S(1)} %slice.5342), channel_id=2, replica_groups=mesh['section'=4,'obs'=8] {'obs'}, dimensions={0}, use_global_device_ids=true | all-gather | bytes 184320 | tf_op jit(solution)/shard_map/while/body/eval_jaxpr/all_gather | solution.py:144
  244.0 17.5 %psum.19 = f32[1,2]{1,0:T(1,128)S(1)} all-reduce(f32[1,2]{1,0:T(1,128)S(1)} %maximum_bitcast_fusion.6), channel_id=1, replica_groups=mesh['section'=4,'obs'=8] {'obs'}, use_global_device_ids=true, to_apply=%region_7.8 | all-reduce | flops 2 | bytes 16 | tf_op jit(solution)/shard_map/while/body/eval_jaxpr/psum | solution.py:157
  264.4 3.4 all-to-all-start
  269.0 4.4 all-to-all-done
  279.6 13.4 %collective-permute-start = (f32[1,230,256]{2,1,0:T(8,128)S(1)}, f32[1,230,256]{2,1,0:T(8,128)S(1)}, u32[]{:S(2)}, u32[]{:S(2)}) collective-permute-start(f32[1,230,256]{2,1,0:T(8,128)S(1)} %pad_maximum_fusion.2), channel_id=1, source_target_pairs={{0,8},{8,16},{16,24},{1,9},{9,17},{17,25},{2,10},{10,18},{18,26},{... | collective-permute-start | bytes 706568 | tf_op jit(solution)/shard_map/while/body/eval_jaxpr/ppermute | solution.py:14
  293.4 5.9 dynamic_update_slice.31
  303.9 3.3 all-to-all-start.1
  309.7 24.8 %all-gather.3 = f32[8,20,256]{2,1,0:T(8,128)S(1)} all-gather(f32[1,20,256]{2,1,0:T(8,128)S(1)} %slice.5342), channel_id=2, replica_groups=mesh['section'=4,'obs'=8] {'obs'}, dimensions={0}, use_global_device_ids=true | all-gather | bytes 184320 | tf_op jit(solution)/shard_map/while/body/eval_jaxpr/all_gather | solution.py:144
  341.3 17.6 %psum.19 = f32[1,2]{1,0:T(1,128)S(1)} all-reduce(f32[1,2]{1,0:T(1,128)S(1)} %maximum_bitcast_fusion.6), channel_id=1, replica_groups=mesh['section'=4,'obs'=8] {'obs'}, use_global_device_ids=true, to_apply=%region_7.8 | all-reduce | flops 2 | bytes 16 | tf_op jit(solution)/shard_map/while/body/eval_jaxpr/psum | solution.py:157
  361.8 3.4 all-to-all-start
  366.4 4.4 all-to-all-done
  377.0 13.1 %collective-permute-start = (f32[1,230,256]{2,1,0:T(8,128)S(1)}, f32[1,230,256]{2,1,0:T(8,128)S(1)}, u32[]{:S(2)}, u32[]{:S(2)}) collective-permute-start(f32[1,230,256]{2,1,0:T(8,128)S(1)} %pad_maximum_fusion.2), channel_id=1, source_target_pairs={{0,8},{8,16},{16,24},{1,9},{9,17},{17,25},{2,10},{10,18},{18,26},{... | collective-permute-start | bytes 706568 | tf_op jit(solution)/shard_map/while/body/eval_jaxpr/ppermute | solution.py:14
  390.5 5.9 dynamic_update_slice.31
  401.0 3.3 all-to-all-start.1
  406.7 24.9 %all-gather.3 = f32[8,20,256]{2,1,0:T(8,128)S(1)} all-gather(f32[1,20,256]{2,1,0:T(8,128)S(1)} %slice.5342), channel_id=2, replica_groups=mesh['section'=4,'obs'=8] {'obs'}, dimensions={0}, use_global_device_ids=true | all-gather | bytes 184320 | tf_op jit(solution)/shard_map/while/body/eval_jaxpr/all_gather | solution.py:144
  438.4 17.2 %psum.19 = f32[1,2]{1,0:T(1,128)S(1)} all-reduce(f32[1,2]{1,0:T(1,128)S(1)} %maximum_bitcast_fusion.6), channel_id=1, replica_groups=mesh['section'=4,'obs'=8] {'obs'}, use_global_device_ids=true, to_apply=%region_7.8 | all-reduce | flops 2 | bytes 16 | tf_op jit(solution)/shard_map/while/body/eval_jaxpr/psum | solution.py:157
  458.5 3.4 all-to-all-start
  463.2 4.4 all-to-all-done
  473.8 13.4 %collective-permute-start = (f32[1,230,256]{2,1,0:T(8,128)S(1)}, f32[1,230,256]{2,1,0:T(8,128)S(1)}, u32[]{:S(2)}, u32[]{:S(2)}) collective-permute-start(f32[1,230,256]{2,1,0:T(8,128)S(1)} %pad_maximum_fusion.2), channel_id=1, source_target_pairs={{0,8},{8,16},{16,24},{1,9},{9,17},{17,25},{2,10},{10,18},{18,26},{... | collective-permute-start | bytes 706568 | tf_op jit(solution)/shard_map/while/body/eval_jaxpr/ppermute | solution.py:14
  487.5 5.9 dynamic_update_slice.31
  503.8 24.8 %all-gather.3 = f32[8,20,256]{2,1,0:T(8,128)S(1)} all-gather(f32[1,20,256]{2,1,0:T(8,128)S(1)} %slice.5342), channel_id=2, replica_groups=mesh['section'=4,'obs'=8] {'obs'}, dimensions={0}, use_global_device_ids=true | all-gather | bytes 184320 | tf_op jit(solution)/shard_map/while/body/eval_jaxpr/all_gather | solution.py:144
  535.4 17.5 %psum.19 = f32[1,2]{1,0:T(1,128)S(1)} all-reduce(f32[1,2]{1,0:T(1,128)S(1)} %maximum_bitcast_fusion.6), channel_id=1, replica_groups=mesh['section'=4,'obs'=8] {'obs'}, use_global_device_ids=true, to_apply=%region_7.8 | all-reduce | flops 2 | bytes 16 | tf_op jit(solution)/shard_map/while/body/eval_jaxpr/psum | solution.py:157
  555.8 3.4 all-to-all-start
  560.4 4.4 all-to-all-done
  571.0 13.2 %collective-permute-start = (f32[1,230,256]{2,1,0:T(8,128)S(1)}, f32[1,230,256]{2,1,0:T(8,128)S(1)}, u32[]{:S(2)}, u32[]{:S(2)}) collective-permute-start(f32[1,230,256]{2,1,0:T(8,128)S(1)} %pad_maximum_fusion.2), channel_id=1, source_target_pairs={{0,8},{8,16},{16,24},{1,9},{9,17},{17,25},{2,10},{10,18},{18,26},{... | collective-permute-start | bytes 706568 | tf_op jit(solution)/shard_map/while/body/eval_jaxpr/ppermute | solution.py:14
  584.6 5.9 dynamic_update_slice.31
  600.9 24.5 %all-gather.3 = f32[8,20,256]{2,1,0:T(8,128)S(1)} all-gather(f32[1,20,256]{2,1,0:T(8,128)S(1)} %slice.5342), channel_id=2, replica_groups=mesh['section'=4,'obs'=8] {'obs'}, dimensions={0}, use_global_device_ids=true | all-gather | bytes 184320 | tf_op jit(solution)/shard_map/while/body/eval_jaxpr/all_gather | solution.py:144
  632.1 18.0 %psum.19 = f32[1,2]{1,0:T(1,128)S(1)} all-reduce(f32[1,2]{1,0:T(1,128)S(1)} %maximum_bitcast_fusion.6), channel_id=1, replica_groups=mesh['section'=4,'obs'=8] {'obs'}, use_global_device_ids=true, to_apply=%region_7.8 | all-reduce | flops 2 | bytes 16 | tf_op jit(solution)/shard_map/while/body/eval_jaxpr/psum | solution.py:157
  652.9 3.4 all-to-all-start
  657.6 4.4 all-to-all-done
  668.2 13.1 %collective-permute-start = (f32[1,230,256]{2,1,0:T(8,128)S(1)}, f32[1,230,256]{2,1,0:T(8,128)S(1)}, u32[]{:S(2)}, u32[]{:S(2)}) collective-permute-start(f32[1,230,256]{2,1,0:T(8,128)S(1)} %pad_maximum_fusion.2), channel_id=1, source_target_pairs={{0,8},{8,16},{16,24},{1,9},{9,17},{17,25},{2,10},{10,18},{18,26},{... | collective-permute-start | bytes 706568 | tf_op jit(solution)/shard_map/while/body/eval_jaxpr/ppermute | solution.py:14
  681.7 5.9 dynamic_update_slice.31
  (632 shorter events, 155.7 us)
Async XLA Ops:
  2.2 0.7 copy-start.4
  2.3 0.7 copy-start.5
  2.3 0.7 copy-start.6
  7.5 60.4 %all-to-all-start.1 = ((f32[1,8,8]{2,0,1:T(1,128)}), f32[1,8,8]{2,0,1:T(1,128)S(1)}, u32[]{:S(2)}, u32[]{:S(2)}) async-start(f32[1,8,8]{2,0,1:T(1,128)} %bitcast.2462), calls=%async_computation.1 | async-start | bytes 8192 | tf_op jit(solution)/shard_map/while/body/eval_jaxpr/all_to_all | solution.py:161
  68.0 9.1 %all-to-all-start = ((f32[1,8,8,230]{3,2,0,1:T(8,128)}), f32[1,8,8,230]{3,2,0,1:T(8,128)S(1)}, u32[]{:S(2)}, u32[]{:S(2)}) async-start(f32[1,8,8,230]{3,2,0,1:T(8,128)} %convolution_bitcast_fusion.4), calls=%async_computation | async-start | bytes 131072 | tf_op jit(solution)/shard_map/while/body/eval_jaxpr/all_to_all | solution.py:160
  77.4 0.6 copy-start
  78.8 0.7 slice-start
  80.7 0.7 copy-start.1
  83.2 22.0 %collective-permute-start = (f32[1,230,256]{2,1,0:T(8,128)S(1)}, f32[1,230,256]{2,1,0:T(8,128)S(1)}, u32[]{:S(2)}, u32[]{:S(2)}) collective-permute-start(f32[1,230,256]{2,1,0:T(8,128)S(1)} %pad_maximum_fusion.2), channel_id=1, source_target_pairs={{0,8},{8,16},{16,24},{1,9},{9,17},{17,25},{2,10},{10,18},{18,26},{... | collective-permute-start | bytes 706568 | tf_op jit(solution)/shard_map/while/body/eval_jaxpr/ppermute | solution.py:14
  109.8 57.8 %all-to-all-start.1 = ((f32[1,8,8]{2,0,1:T(1,128)}), f32[1,8,8]{2,0,1:T(1,128)S(1)}, u32[]{:S(2)}, u32[]{:S(2)}) async-start(f32[1,8,8]{2,0,1:T(1,128)} %bitcast.2462), calls=%async_computation.1 | async-start | bytes 8192 | tf_op jit(solution)/shard_map/while/body/eval_jaxpr/all_to_all | solution.py:161
  167.6 9.1 %all-to-all-start = ((f32[1,8,8,230]{3,2,0,1:T(8,128)}), f32[1,8,8,230]{3,2,0,1:T(8,128)S(1)}, u32[]{:S(2)}, u32[]{:S(2)}) async-start(f32[1,8,8,230]{3,2,0,1:T(8,128)} %convolution_bitcast_fusion.4), calls=%async_computation | async-start | bytes 131072 | tf_op jit(solution)/shard_map/while/body/eval_jaxpr/all_to_all | solution.py:160
  177.1 0.6 copy-start
  178.5 0.7 slice-start
  180.4 0.7 copy-start.1
  182.9 19.4 %collective-permute-start = (f32[1,230,256]{2,1,0:T(8,128)S(1)}, f32[1,230,256]{2,1,0:T(8,128)S(1)}, u32[]{:S(2)}, u32[]{:S(2)}) collective-permute-start(f32[1,230,256]{2,1,0:T(8,128)S(1)} %pad_maximum_fusion.2), channel_id=1, source_target_pairs={{0,8},{8,16},{16,24},{1,9},{9,17},{17,25},{2,10},{10,18},{18,26},{... | collective-permute-start | bytes 706568 | tf_op jit(solution)/shard_map/while/body/eval_jaxpr/ppermute | solution.py:14
  206.9 57.5 %all-to-all-start.1 = ((f32[1,8,8]{2,0,1:T(1,128)}), f32[1,8,8]{2,0,1:T(1,128)S(1)}, u32[]{:S(2)}, u32[]{:S(2)}) async-start(f32[1,8,8]{2,0,1:T(1,128)} %bitcast.2462), calls=%async_computation.1 | async-start | bytes 8192 | tf_op jit(solution)/shard_map/while/body/eval_jaxpr/all_to_all | solution.py:161
  264.4 9.1 %all-to-all-start = ((f32[1,8,8,230]{3,2,0,1:T(8,128)}), f32[1,8,8,230]{3,2,0,1:T(8,128)S(1)}, u32[]{:S(2)}, u32[]{:S(2)}) async-start(f32[1,8,8,230]{3,2,0,1:T(8,128)} %convolution_bitcast_fusion.4), calls=%async_computation | async-start | bytes 131072 | tf_op jit(solution)/shard_map/while/body/eval_jaxpr/all_to_all | solution.py:160
  273.8 0.6 copy-start
  275.2 0.7 slice-start
  277.1 0.7 copy-start.1
  279.6 19.7 %collective-permute-start = (f32[1,230,256]{2,1,0:T(8,128)S(1)}, f32[1,230,256]{2,1,0:T(8,128)S(1)}, u32[]{:S(2)}, u32[]{:S(2)}) collective-permute-start(f32[1,230,256]{2,1,0:T(8,128)S(1)} %pad_maximum_fusion.2), channel_id=1, source_target_pairs={{0,8},{8,16},{16,24},{1,9},{9,17},{17,25},{2,10},{10,18},{18,26},{... | collective-permute-start | bytes 706568 | tf_op jit(solution)/shard_map/while/body/eval_jaxpr/ppermute | solution.py:14
  303.9 57.8 %all-to-all-start.1 = ((f32[1,8,8]{2,0,1:T(1,128)}), f32[1,8,8]{2,0,1:T(1,128)S(1)}, u32[]{:S(2)}, u32[]{:S(2)}) async-start(f32[1,8,8]{2,0,1:T(1,128)} %bitcast.2462), calls=%async_computation.1 | async-start | bytes 8192 | tf_op jit(solution)/shard_map/while/body/eval_jaxpr/all_to_all | solution.py:161
  361.8 9.1 %all-to-all-start = ((f32[1,8,8,230]{3,2,0,1:T(8,128)}), f32[1,8,8,230]{3,2,0,1:T(8,128)S(1)}, u32[]{:S(2)}, u32[]{:S(2)}) async-start(f32[1,8,8,230]{3,2,0,1:T(8,128)} %convolution_bitcast_fusion.4), calls=%async_computation | async-start | bytes 131072 | tf_op jit(solution)/shard_map/while/body/eval_jaxpr/all_to_all | solution.py:160
  371.2 0.6 copy-start
  372.6 0.7 slice-start
  374.5 0.7 copy-start.1
  377.0 19.4 %collective-permute-start = (f32[1,230,256]{2,1,0:T(8,128)S(1)}, f32[1,230,256]{2,1,0:T(8,128)S(1)}, u32[]{:S(2)}, u32[]{:S(2)}) collective-permute-start(f32[1,230,256]{2,1,0:T(8,128)S(1)} %pad_maximum_fusion.2), channel_id=1, source_target_pairs={{0,8},{8,16},{16,24},{1,9},{9,17},{17,25},{2,10},{10,18},{18,26},{... | collective-permute-start | bytes 706568 | tf_op jit(solution)/shard_map/while/body/eval_jaxpr/ppermute | solution.py:14
  401.0 57.5 %all-to-all-start.1 = ((f32[1,8,8]{2,0,1:T(1,128)}), f32[1,8,8]{2,0,1:T(1,128)S(1)}, u32[]{:S(2)}, u32[]{:S(2)}) async-start(f32[1,8,8]{2,0,1:T(1,128)} %bitcast.2462), calls=%async_computation.1 | async-start | bytes 8192 | tf_op jit(solution)/shard_map/while/body/eval_jaxpr/all_to_all | solution.py:161
  458.5 9.1 %all-to-all-start = ((f32[1,8,8,230]{3,2,0,1:T(8,128)}), f32[1,8,8,230]{3,2,0,1:T(8,128)S(1)}, u32[]{:S(2)}, u32[]{:S(2)}) async-start(f32[1,8,8,230]{3,2,0,1:T(8,128)} %convolution_bitcast_fusion.4), calls=%async_computation | async-start | bytes 131072 | tf_op jit(solution)/shard_map/while/body/eval_jaxpr/all_to_all | solution.py:160
  468.0 0.6 copy-start
  469.4 0.7 slice-start
  471.3 0.7 copy-start.1
  473.8 19.7 %collective-permute-start = (f32[1,230,256]{2,1,0:T(8,128)S(1)}, f32[1,230,256]{2,1,0:T(8,128)S(1)}, u32[]{:S(2)}, u32[]{:S(2)}) collective-permute-start(f32[1,230,256]{2,1,0:T(8,128)S(1)} %pad_maximum_fusion.2), channel_id=1, source_target_pairs={{0,8},{8,16},{16,24},{1,9},{9,17},{17,25},{2,10},{10,18},{18,26},{... | collective-permute-start | bytes 706568 | tf_op jit(solution)/shard_map/while/body/eval_jaxpr/ppermute | solution.py:14
  498.1 57.7 %all-to-all-start.1 = ((f32[1,8,8]{2,0,1:T(1,128)}), f32[1,8,8]{2,0,1:T(1,128)S(1)}, u32[]{:S(2)}, u32[]{:S(2)}) async-start(f32[1,8,8]{2,0,1:T(1,128)} %bitcast.2462), calls=%async_computation.1 | async-start | bytes 8192 | tf_op jit(solution)/shard_map/while/body/eval_jaxpr/all_to_all | solution.py:161
  555.8 9.1 %all-to-all-start = ((f32[1,8,8,230]{3,2,0,1:T(8,128)}), f32[1,8,8,230]{3,2,0,1:T(8,128)S(1)}, u32[]{:S(2)}, u32[]{:S(2)}) async-start(f32[1,8,8,230]{3,2,0,1:T(8,128)} %convolution_bitcast_fusion.4), calls=%async_computation | async-start | bytes 131072 | tf_op jit(solution)/shard_map/while/body/eval_jaxpr/all_to_all | solution.py:160
  565.2 0.6 copy-start
  566.6 0.7 slice-start
  568.5 0.7 copy-start.1
  571.0 19.5 %collective-permute-start = (f32[1,230,256]{2,1,0:T(8,128)S(1)}, f32[1,230,256]{2,1,0:T(8,128)S(1)}, u32[]{:S(2)}, u32[]{:S(2)}) collective-permute-start(f32[1,230,256]{2,1,0:T(8,128)S(1)} %pad_maximum_fusion.2), channel_id=1, source_target_pairs={{0,8},{8,16},{16,24},{1,9},{9,17},{17,25},{2,10},{10,18},{18,26},{... | collective-permute-start | bytes 706568 | tf_op jit(solution)/shard_map/while/body/eval_jaxpr/ppermute | solution.py:14
  595.1 57.8 %all-to-all-start.1 = ((f32[1,8,8]{2,0,1:T(1,128)}), f32[1,8,8]{2,0,1:T(1,128)S(1)}, u32[]{:S(2)}, u32[]{:S(2)}) async-start(f32[1,8,8]{2,0,1:T(1,128)} %bitcast.2462), calls=%async_computation.1 | async-start | bytes 8192 | tf_op jit(solution)/shard_map/while/body/eval_jaxpr/all_to_all | solution.py:161
  652.9 9.1 %all-to-all-start = ((f32[1,8,8,230]{3,2,0,1:T(8,128)}), f32[1,8,8,230]{3,2,0,1:T(8,128)S(1)}, u32[]{:S(2)}, u32[]{:S(2)}) async-start(f32[1,8,8,230]{3,2,0,1:T(8,128)} %convolution_bitcast_fusion.4), calls=%async_computation | async-start | bytes 131072 | tf_op jit(solution)/shard_map/while/body/eval_jaxpr/all_to_all | solution.py:160
  662.4 0.6 copy-start
  663.8 0.7 slice-start
  665.7 0.7 copy-start.1
  668.2 19.4 %collective-permute-start = (f32[1,230,256]{2,1,0:T(8,128)S(1)}, f32[1,230,256]{2,1,0:T(8,128)S(1)}, u32[]{:S(2)}, u32[]{:S(2)}) collective-permute-start(f32[1,230,256]{2,1,0:T(8,128)S(1)} %pad_maximum_fusion.2), channel_id=1, source_target_pairs={{0,8},{8,16},{16,24},{1,9},{9,17},{17,25},{2,10},{10,18},{18,26},{... | collective-permute-start | bytes 706568 | tf_op jit(solution)/shard_map/while/body/eval_jaxpr/ppermute | solution.py:14
  687.6 0.9 copy-start.2
  687.6 0.9 copy-start.3
